TPU v7x, 32 devices: a whole 2x2x4 slice. The times are simulated.
32 devices in a mesh: grid: 8 (over y, x, core), ipts: 4 (over z).
Axes of the slice: x: 2, y: 2, z: 4, core: 2. Of those that a mesh axis runs over, the one named last changes fastest.
Arguments:
- orbitals: bfloat16 [16384, 1024], P(('grid', 'ipts')), may hold values from -1.1953125 to 1.1953125
- targets: bfloat16 [16384, 256], P(('grid', 'ipts')), may hold values from -6 to 6
- points: int32 [4, 1024], P('ipts', 'grid'), may hold values from 0 to 16383, as said below
- potential: bfloat16 [16384, 4096], P('grid', 'ipts'), may hold values from -0.09375 to 0.09375
Outputs:
- exchanged: bfloat16 [16384, 256], P(('grid', 'ipts'))
Inputs may be any that keep to these rules, and one draw needn't show every extreme that they name: Indices are distinct over all groups; each row of points rises strictly, and its entries k * 128 to (k + 1) * 128 - 1 lie in grid rows k * 2048 to (k + 1) * 2048 - 1.
All inputs are finite; a program needn't handle non-finite values.
Results may differ from a plain program's by a relative error of at most 0.0049.
Values may be sent and summed in bfloat16 or wider, within the bound.
A program may use at most 128 MiB of HBM per device.

v0:
```python
import jax
import jax.numpy as jnp
from jax import lax
from jax.sharding import PartitionSpec as P


def local(orbitals, targets, points, potential):
    groups = lax.axis_size("ipts")
    own_rows = orbitals.shape[0]
    slab_length = own_rows * groups
    slab_start = lax.axis_index("grid") * slab_length
    whole_slab = lax.all_gather(orbitals, "ipts", axis=0, tiled=True)
    every_group = lax.all_gather(points, "ipts", axis=0, tiled=True)
    orbital_values = jnp.take(whole_slab, points[0] - slab_start, axis=0)
    offset = every_group - (slab_start + lax.axis_index("ipts") * own_rows)
    inside = (offset >= 0) & (offset < own_rows)
    clipped = jnp.clip(offset, 0, own_rows - 1)
    picked = jnp.take(targets, clipped, axis=0) * inside[:, :, None].astype(targets.dtype)
    summed = lax.psum_scatter(picked, "ipts", scatter_dimension=0, tiled=True).astype(jnp.float32)
    target_values = summed[0].astype(jnp.bfloat16)
    orbital_piece = lax.all_gather(orbital_values, "grid", axis=0, tiled=True)
    target_piece = lax.all_gather(target_values, "grid", axis=0, tiled=True)
    products = lax.dot_general(
        whole_slab, orbital_piece, (((1,), (1,)), ((), ())), preferred_element_type=jnp.float32
    )
    weighted = (potential * products).astype(jnp.bfloat16)
    group_total = jnp.dot(weighted, target_piece, preferred_element_type=jnp.float32)
    summed_rows = lax.psum_scatter(group_total, "ipts", scatter_dimension=0, tiled=True)
    return (-summed_rows).astype(jnp.bfloat16)


def solution(mesh):
    placed = (
        P(("grid", "ipts"), None),
        P(("grid", "ipts"), None),
        P("ipts", "grid"),
        P("grid", "ipts"),
    )
    return jax.shard_map(
        local, mesh=mesh, in_specs=placed, out_specs=P(("grid", "ipts"), None), check_vma=False
    )
```

profile of v0, /device:TPU:0, one launch (start us, length us, event | category | flops | bytes accessed | tf_op | source)
XLA Modules:
  0.0 204.3 jit_solution(11490571779918535644)
XLA Ops:
  6.5 0.0 copy-start
  6.5 0.0 all-gather.5.cloned.1.call-start
  6.5 0.7 all-gather.5.cloned.1.call-update
  7.3 0.0 reduce-scatter.3.cloned.1.call-start
  7.3 12.8 %all-gather.1 = s32[4,1,128]{2,1,0:T(1,128)S(1)} all-gather(s32[1,1,128]{2,1,0:T(1,128)} %bitcast.29), channel_id=1, replica_groups=mesh['grid'=8,'ipts'=4] {'ipts'}, dimensions={0}, use_global_device_ids=true | all-gather | bytes 2560 | tf_op jit(solution)/shard_map/all_gather | solution.py:13
  20.2 0.0 copy-done
  20.2 2.0 gather_fusion.1
  22.2 0.9 select_multiply_fusion
  23.1 0.0 reduce-scatter.3.cloned.1.call-update
  23.1 0.0 all-gather.7.cloned.1.call-start
  23.2 0.0 copy-done.1
  23.2 69.2 %all-gather.5.cloned.1.call-done = bf16[2048,1024]{1,0:T(8,128)(2,1)} async-done(((bf16[512,1024]{1,0:T(8,128)(2,1)}), bf16[2048,1024]{1,0:T(8,128)(2,1)}) %all-gather.5.cloned.1.call-update) | async-done | bytes 4194320 | tf_op jit(solution)/shard_map/all_gather | solution.py:12
  92.4 3.8 %gather_fusion = bf16[128,1024]{1,0:T(8,128)(2,1)S(1)} fusion(bf16[2048,1024]{1,0:T(8,128)(2,1)} %all-gather.5.cloned.1.call-done, s32[1024]{0:T(1024)S(1)} %pad_clamp_fusion.1), kind=kCustom, calls=%fused_computation | custom fusion | bytes 524800 | tf_op jit(solution)/shard_map/jit(_take)/gather | solution.py:14
  96.2 0.8 broadcast_select_fusion
  97.0 0.0 all-gather.7.cloned.1.call-update
  97.0 0.0 reduce-scatter.5.cloned.1.call-start
  97.0 6.5 %copy.5 = bf16[2048,1024]{0,1:T(8,128)(2,1)} copy(bf16[2048,1024]{1,0:T(8,128)(2,1)} %param.7) | data formatting | bytes 8388608 | tf_op args[3]
  103.6 9.6 %reduce-scatter.3.cloned.1.call-done = bf16[1,128,256]{2,1,0:T(8,128)(2,1)} async-done(((bf16[4,128,256]{2,1,0:T(8,128)(2,1)}), bf16[1,128,256]{2,1,0:T(8,128)(2,1)}) %reduce-scatter.3.cloned.1.call-update) | async-done | bytes 65552 | tf_op jit(solution)/shard_map/reduce_scatter | solution.py:19
  113.2 10.1 %all-gather = bf16[1,1024,256]{2,1,0:T(8,128)(2,1)S(1)} all-gather(bf16[1,128,256]{2,1,0:T(8,128)(2,1)} %reduce-scatter.3.cloned.1.call-done), channel_id=2, replica_groups=mesh['grid'=8,'ipts'=4] {'grid'}, dimensions={1}, use_global_device_ids=true | all-gather | bytes 589824 | tf_op jit(solution)/shard_map/all_gather | solution.py:22
  123.3 17.8 %all-gather.7.cloned.1.call-done = bf16[1024,1024]{1,0:T(8,128)(2,1)} async-done(((bf16[128,1024]{1,0:T(8,128)(2,1)}), bf16[1024,1024]{1,0:T(8,128)(2,1)}) %all-gather.7.cloned.1.call-update) | async-done | bytes 2097168 | tf_op jit(solution)/shard_map/all_gather | solution.py:21
  141.1 11.0 %fusion.1 = f32[2048,256]{1,0:T(8,128)} fusion(bf16[2048,1024]{0,1:T(8,128)(2,1)} %copy.5, bf16[1024,1024]{1,0:T(8,128)(2,1)} %all-gather.7.cloned.1.call-done, bf16[2048,1024]{1,0:T(8,128)(2,1)} %all-gather.5.cloned.1.call-done, bf16[1,1024,256]{2,1,0:T(8,128)(2,1)S(1)} %all-gather), kind=kOutput, calls=%fused_computation.4 | convolution fusion | flops 5375000576 | bytes 13107200 | tf_op jit(solution)/shard_map/dot_general | solution.py:27
  152.1 0.0 reduce-scatter.5.cloned.1.call-update
  152.2 43.8 %reduce-scatter.5.cloned.1.call-done = f32[512,256]{1,0:T(8,128)} async-done(((f32[2048,256]{1,0:T(8,128)}), f32[512,256]{1,0:T(8,128)}) %reduce-scatter.5.cloned.1.call-update) | async-done | bytes 524304 | tf_op jit(solution)/shard_map/reduce_scatter | solution.py:28
  195.9 1.8 negate_convert_fusion
  (10 shorter events, 0.1 us)
Async XLA Ops:
  6.5 13.6 %copy-start = (bf16[512,256]{1,0:T(8,128)(2,1)S(1)}, bf16[512,256]{1,0:T(8,128)(2,1)}, u32[]{:S(2)}) copy-start(bf16[512,256]{1,0:T(8,128)(2,1)} %param.5) | copy-start | bytes 786436
  6.5 16.6 %copy-start.1 = (s32[1,128]{1,0:T(1,128)S(1)}, s32[1,128]{1,0:T(1,128)}, u32[]{:S(2)}) copy-start(s32[1,128]{1,0:T(1,128)} %param.6) | copy-start | bytes 1540
  6.5 85.9 %all-gather.5.cloned.1.call-start = ((), (), s32[]{:S(2)}) async-start(), calls=%async_computation.2 | async-start | bytes 5242880 | tf_op jit(solution)/shard_map/all_gather | solution.py:12
  7.3 105.9 %reduce-scatter.3.cloned.1.call-start = ((), (), s32[]{:S(2)}) async-start(), calls=%async_computation.4 | async-start | bytes 327680 | tf_op jit(solution)/shard_map/reduce_scatter | solution.py:19
  23.1 118.0 %all-gather.7.cloned.1.call-start = ((), (), s32[]{:S(2)}) async-start(), calls=%async_computation.3 | async-start | bytes 2359296 | tf_op jit(solution)/shard_map/all_gather | solution.py:21
  97.0 98.9 %reduce-scatter.5.cloned.1.call-start = ((), (), s32[]{:S(2)}) async-start(), calls=%async_computation.5 | async-start | bytes 2621440 | tf_op jit(solution)/shard_map/reduce_scatter | solution.py:28
Sparse Core Ops, SparseCore 0:
  8.9 83.4 all-gather.4
  94.7 18.4 reduce-scatter.2
  115.1 25.9 all-gather.6
  152.3 43.6 reduce-scatter.4
where the time goes:
time: 205 us; the launch traced here: 204 us
  waiting for transfers between devices  141 us (69%)
  blocking collectives  22.9 us (11%)
  between operations  13.2 us (6%)
  local copies, waits for them, and re-layouts  12.3 us (6%)
  matrix products  11 us (5%)
  other arithmetic  3.55 us (2%)
    all_gather x1, waiting for transfers between devices, local(): whole_slab = lax.all_gather(orbitals, 'ipts', axis=0, tiled=True)  69.2 us
    reduce_scatter x1, waiting for transfers between devices, local(): lax.psum_scatter(group_total, 'ipts', scatter_dimension=0, tiled=True)  43.8 us
    all_gather x1, waiting for transfers between devices, local(): orbital_piece = lax.all_gather(orbital_values, 'grid', axis=0, tiled=True)  17.8 us
    all_gather x1, blocking collectives, local(): every_group = lax.all_gather(points, 'ipts', axis=0, tiled=True)  12.8 us
    dot_general x1, matrix products, local(): jnp.dot(weighted, target_piece, preferred_element_type=jnp.float32)  11 us
    all_gather x1, blocking collectives, local(): target_piece = lax.all_gather(target_values, 'grid', axis=0, tiled=True)  10.1 us
    reduce_scatter x1, waiting for transfers between devices, local(): lax.psum_scatter(picked, 'ipts', scatter_dimension=0, tiled=True)  9.59 us
    unnamed x6, local copies, waits for them, and re-layouts  6.53 us
  transfers between devices with their start and end apart: 4, of which 4 were waited for; matrix products, arithmetic and copies ran while one was open for 7% of the time, Pallas kernels for 0%

commit v1 on v0

v1 whole, which is shorter than its diff:
```python
import functools

import jax
import jax.numpy as jnp
from jax import lax
from jax.experimental import pallas as pl
from jax.experimental.pallas import tpu as pltpu
from jax.sharding import PartitionSpec as P

MESH = pl.DeviceIdType.MESH
WIDTH = 256


def kernel(groups, slabs, pieces, orbitals, targets, points, potential, out,
           slab, orbital_values, target_values, weights, target_rows, every_group, picked, landed,
           total, leaving, arriving,
           local_sem, up_sem, down_sem, row_sem, grid_send, grid_recv, index_send, index_recv,
           pick_send, pick_recv, value_send, value_recv, sum_send, sum_recv):
    g = lax.axis_index("grid")
    z = lax.axis_index("ipts")
    rows, norb = orbitals.shape
    nj = targets.shape[1]
    count = points.shape[1]
    cut = norb // pieces

    def at(grid, group):
        return {"grid": grid, "ipts": group}

    def other(base, step, size):
        return lax.rem(base + step, size)

    own = [
        pltpu.make_async_copy(
            orbitals.at[:, pl.ds(k * cut, cut)], slab.at[z, :, pl.ds(k * cut, cut)], local_sem.at[k])
        for k in range(pieces)
    ]
    own_targets = pltpu.make_async_copy(targets, target_rows, local_sem.at[pieces])
    own_points = pltpu.make_async_copy(points, every_group.at[0], local_sem.at[pieces + 1])
    own_weights = pltpu.make_async_copy(potential, weights, local_sem.at[pieces + 2])
    own_points.start()
    for copy in own:
        copy.start()
    own_targets.start()
    own_weights.start()

    barrier = pltpu.get_barrier_semaphore()
    for step in range(1, groups):
        pl.semaphore_signal(barrier, inc=1, device_id=at(g, other(z, step, groups)), device_id_type=MESH)
    for step in range(1, slabs):
        pl.semaphore_signal(barrier, inc=1, device_id=at(other(g, step, slabs), z), device_id_type=MESH)
    pl.semaphore_wait(barrier, groups + slabs - 2)

    def line_copy(k, chunk, sem, target):
        block = slab.at[chunk, :, pl.ds(k * cut, cut)]
        return pltpu.make_async_remote_copy(
            src_ref=block, dst_ref=block, send_sem=sem, recv_sem=row_sem.at[k, chunk],
            device_id=at(g, target), device_id_type=MESH)

    def up(k, d):
        return (z - d >= 0) & (z + 1 < groups), line_copy(
            k, jnp.maximum(z - d, 0), up_sem.at[k, d], jnp.minimum(z + 1, groups - 1))

    def down(k, d):
        return (z + d < groups) & (z >= 1), line_copy(
            k, jnp.minimum(z + d, groups - 1), down_sem.at[k, d], jnp.maximum(z - 1, 0))

    def send_line(k, d):
        for valid, copy in (up(k, d), down(k, d)):
            pl.when(valid)(copy.start)

    def await_line(k, d):
        pl.when(z - d >= 0)(lambda: line_copy(k, jnp.maximum(z - d, 0), up_sem.at[k, 0], z).wait_recv())
        pl.when(z + d < groups)(
            lambda: line_copy(k, jnp.minimum(z + d, groups - 1), up_sem.at[k, 0], z).wait_recv())

    own[0].wait()
    send_line(0, 0)
    own_points.wait()
    index_copies = [
        pltpu.make_async_remote_copy(
            src_ref=every_group.at[0], dst_ref=every_group.at[step],
            send_sem=index_send.at[step - 1], recv_sem=index_recv.at[step - 1],
            device_id=at(g, other(z, step, groups)), device_id_type=MESH)
        for step in range(1, groups)
    ]
    for copy in index_copies:
        copy.start()

    slab_start = g * rows * groups

    def chosen(indices, start, length):
        place = lax.broadcasted_iota(jnp.int32, (length, count), 0) + start
        return (place == indices).astype(jnp.float32).astype(jnp.bfloat16)

    def pick(indices, start, block):
        return lax.dot_general(
            chosen(indices, start, block.shape[0]), block, (((0,), (0,)), ((), ())),
            preferred_element_type=jnp.float32)

    own_targets.wait()
    own_start = slab_start + z * rows
    pick_copies = []
    own_pick = pick(every_group[0], own_start, target_rows[...])
    for step in range(1, groups):
        index_copies[step - 1].wait()
        picked[step - 1] = pick(every_group[step], own_start, target_rows[...]).astype(jnp.bfloat16)
        copy = pltpu.make_async_remote_copy(
            src_ref=picked.at[step - 1], dst_ref=landed.at[step - 1],
            send_sem=pick_send.at[step - 1], recv_sem=pick_recv.at[step - 1],
            device_id=at(g, other(z, groups - step, groups)), device_id_type=MESH)
        copy.start()
        pick_copies.append(copy)

    place = pl.ds(pl.multiple_of(g * count, count), count)
    grid_copies = []

    def spread(ref, sends, recvs):
        copies = [
            pltpu.make_async_remote_copy(
                src_ref=ref, dst_ref=ref, send_sem=sends.at[step - 1], recv_sem=recvs.at[step - 1],
                device_id=at(other(g, step, slabs), z), device_id_type=MESH)
            for step in range(1, slabs)
        ]
        for copy in copies:
            copy.start()
        grid_copies.extend(copies)

    for s in range(pieces + groups - 1):
        for d in range(groups):
            k = s - d
            if not 0 <= k < pieces:
                continue
            if d > 0:
                await_line(k, d)
            elif k > 0:
                own[k].wait()
            if d < groups - 1 and s > 0:
                send_line(k, d)
        k = s - (groups - 1)
        if k < 0:
            continue
        columns = pl.ds(k * cut, cut)
        values = jnp.zeros((count, cut), jnp.float32)
        for chunk in range(groups):
            values += pick(every_group[0], slab_start + chunk * rows, slab[chunk, :, columns])
        orbital_values[place, columns] = values.astype(jnp.bfloat16)
        spread(orbital_values.at[place, columns], grid_send.at[k], grid_recv.at[k])
        if k == 0:
            values = own_pick
            for step in range(1, groups):
                pick_copies[step - 1].wait()
                values += landed[step - 1].astype(jnp.float32)
            target_values[place, :] = values.astype(jnp.bfloat16)
            spread(target_values.at[place, :], value_send, value_recv)

    own_weights.wait()
    for copy in grid_copies:
        copy.wait_recv()

    def add_up(chunk):
        total[...] = jnp.zeros_like(total)

        @pl.loop(0, slabs * count // WIDTH)
        def _(b):
            block = pl.ds(pl.multiple_of(b * WIDTH, WIDTH), WIDTH)
            products = lax.dot_general(
                slab[chunk], orbital_values[block, :], (((1,), (1,)), ((), ())),
                preferred_element_type=jnp.float32)
            kernel_rows = weights[pl.ds(pl.multiple_of(chunk * rows, rows), rows), block]
            weighted = (kernel_rows.astype(jnp.float32) * products).astype(jnp.bfloat16)
            total[...] += jnp.dot(weighted, target_values[block, :], preferred_element_type=jnp.float32)

    sum_copies = []
    for n, step in enumerate(range(1, groups)):
        chunk = other(z, step, groups)
        add_up(chunk)
        leaving[n] = total[...].astype(jnp.bfloat16)
        copy = pltpu.make_async_remote_copy(
            src_ref=leaving.at[n], dst_ref=arriving.at[n], send_sem=sum_send.at[n], recv_sem=sum_recv.at[n],
            device_id=at(g, chunk), device_id_type=MESH)
        copy.start()
        sum_copies.append(copy)
    add_up(z)
    summed = total[...]
    for n, copy in enumerate(sum_copies):
        copy.wait_recv()
        summed += arriving[n].astype(jnp.float32)
    out[...] = (-summed).astype(out.dtype)

    for k in range(pieces):
        for d in range(groups - 1):
            for valid, copy in (up(k, d), down(k, d)):
                pl.when(valid)(copy.wait_send)
    for copy in grid_copies + sum_copies:
        copy.wait_send()


def local(orbitals, targets, points, potential):
    groups, slabs = lax.axis_size("ipts"), lax.axis_size("grid")
    rows, norb = orbitals.shape
    nj = targets.shape[1]
    count = points.shape[1]
    pieces = max(norb // 256, 1)
    dma, bf16 = pltpu.SemaphoreType.DMA, jnp.bfloat16
    return pl.pallas_call(
        functools.partial(kernel, groups, slabs, pieces),
        out_shape=jax.ShapeDtypeStruct((rows, nj), bf16),
        in_specs=[pl.BlockSpec(memory_space=pl.ANY)] * 4,
        out_specs=pl.BlockSpec(memory_space=pltpu.VMEM),
        scratch_shapes=[
            pltpu.VMEM((groups, rows, norb), bf16),
            pltpu.VMEM((slabs * count, norb), bf16),
            pltpu.VMEM((slabs * count, nj), bf16),
            pltpu.VMEM(potential.shape, bf16),
            pltpu.VMEM((rows, nj), bf16),
            pltpu.VMEM((groups, 1, count), jnp.int32),
            pltpu.VMEM((groups - 1, count, nj), bf16),
            pltpu.VMEM((groups - 1, count, nj), bf16),
            pltpu.VMEM((rows, nj), jnp.float32),
            pltpu.VMEM((groups - 1, rows, nj), bf16),
            pltpu.VMEM((groups - 1, rows, nj), bf16),
            dma((pieces + 3,)),
            dma((pieces, groups - 1)),
            dma((pieces, groups - 1)),
            dma((pieces, groups)),
            dma((pieces, slabs - 1)),
            dma((pieces, slabs - 1)),
            dma((groups - 1,)),
            dma((groups - 1,)),
            dma((groups - 1,)),
            dma((groups - 1,)),
            dma((slabs - 1,)),
            dma((slabs - 1,)),
            dma((groups - 1,)),
            dma((groups - 1,)),
        ],
        compiler_params=pltpu.CompilerParams(
            collective_id=0, has_side_effects=True, vmem_limit_bytes=60 * 1024 * 1024),
    )(orbitals, targets, points, potential)


def solution(mesh):
    placed = (
        P(("grid", "ipts"), None),
        P(("grid", "ipts"), None),
        P("ipts", "grid"),
        P("grid", "ipts"),
    )
    return jax.shard_map(
        local, mesh=mesh, in_specs=placed, out_specs=P(("grid", "ipts"), None), check_vma=False
    )
```

time: 205 us -> 114 us (0.56)
  the two profiles are of different devices: /device:TPU:0 before, /device:TPU:31 now
where the time goes in v1:
time: 114 us
  Pallas kernels  112 us (98%)
  local copies, waits for them, and re-layouts  1.67 us (1%)
    pallas_call x1, Pallas kernels, local(): pl.pallas_call(functools.partial(kernel, groups, slabs, pieces), out_shap...  112 us

profile of v1, /device:TPU:31, one launch (start us, length us, event | category | flops | bytes accessed | tf_op | source)
XLA Modules:
  0.0 113.8 jit_solution(15452731843167559843)
XLA Ops:
  0.0 112.1 %shard_map.46 = bf16[512,256]{1,0:T(8,128)(2,1)} custom-call(bf16[512,1024]{1,0:T(8,128)(2,1)} %orbitals.1, bf16[512,256]{1,0:T(8,128)(2,1)} %targets.1, s32[1,128]{1,0:T(1,128)} %points.1, bf16[2048,1024]{1,0:T(8,128)(2,1)} %potential.1), custom_call_target="tpu_custom_call" | custom-call | tf_op jit(solution)/shard_map/pallas_call | solution.py:205
  112.1 1.7 %copy.6 = bf16[512,256]{1,0:T(8,128)(2,1)} copy(bf16[512,256]{1,0:T(8,128)(2,1)} %shard_map.46) | data formatting | bytes 524288

commit v2 on v1

--- a/solution.py
+++ b/solution.py
@@ -13,15 +13,23 @@
 
 def kernel(groups, slabs, pieces, orbitals, targets, points, potential, out,
            slab, orbital_values, target_values, weights, target_rows, every_group, picked, landed,
-           total, leaving, arriving,
+           total, leaving, arriving, piece_sum, far_leaving, far_values,
+           guest_orbitals, guest_targets, guest_weights,
            local_sem, up_sem, down_sem, row_sem, grid_send, grid_recv, index_send, index_recv,
-           pick_send, pick_recv, value_send, value_recv, sum_send, sum_recv):
+           pick_send, pick_recv, value_send, value_recv, sum_send, sum_recv,
+           far_send, far_recv, guest_send, guest_recv, pass_send, pass_recv):
     g = lax.axis_index("grid")
     z = lax.axis_index("ipts")
     rows, norb = orbitals.shape
     nj = targets.shape[1]
     count = points.shape[1]
     cut = norb // pieces
+    last = groups - 1
+    edge = (z == 0) | (z == last)
+    hosting = (z == 1) | (z == last - 1)
+    host = jnp.where(z == 0, 1, last - 1)
+    far = jnp.where(z == 0, last, 0)
+    guest_chunk = jnp.where(z == 1, last, 0)
 
     def at(grid, group):
         return {"grid": grid, "ipts": group}
@@ -73,8 +81,16 @@
         pl.when(z + d < groups)(
             lambda: line_copy(k, jnp.minimum(z + d, groups - 1), up_sem.at[k, 0], z).wait_recv())
 
-    own[0].wait()
+    early = min(2, pieces)
+    for copy in own:
+        copy.wait()
     send_line(0, 0)
+
+    @pl.when(edge)
+    def _():
+        for k in range(1, early):
+            send_line(k, 0)
+
     own_points.wait()
     index_copies = [
         pltpu.make_async_remote_copy(
@@ -111,39 +127,104 @@
         copy.start()
         pick_copies.append(copy)
 
+    far_copies = [
+        pltpu.make_async_remote_copy(
+            src_ref=far_leaving.at[:, pl.ds(k * cut, cut)], dst_ref=far_values.at[:, pl.ds(k * cut, cut)],
+            send_sem=far_send.at[k], recv_sem=far_recv.at[k], device_id=at(g, far), device_id_type=MESH)
+        for k in range(pieces)
+    ]
+    weight_copy = pltpu.make_async_remote_copy(
+        src_ref=potential.at[pl.ds(pl.multiple_of(far * rows, rows), rows), :], dst_ref=guest_weights,
+        send_sem=guest_send.at[pieces + 1], recv_sem=guest_recv.at[pieces + 1],
+        device_id=at(g, host), device_id_type=MESH)
+
+    @pl.when(edge)
+    def _():
+        far_group = every_group[jnp.where(z == 0, 1, last)]
+        for k in range(pieces):
+            columns = pl.ds(k * cut, cut)
+            far_leaving[:, columns] = pick(far_group, own_start, slab[z, :, columns]).astype(jnp.bfloat16)
+            far_copies[k].start()
+        for k in range(early, pieces):
+            send_line(k, 0)
+        weight_copy.start()
+
     place = pl.ds(pl.multiple_of(g * count, count), count)
     grid_copies = []
 
-    def spread(ref, sends, recvs):
-        copies = [
+    def spread_copies(ref, sends, recvs):
+        return [
             pltpu.make_async_remote_copy(
                 src_ref=ref, dst_ref=ref, send_sem=sends.at[step - 1], recv_sem=recvs.at[step - 1],
                 device_id=at(other(g, step, slabs), z), device_id_type=MESH)
             for step in range(1, slabs)
         ]
+
+    def spread(ref, sends, recvs):
+        copies = spread_copies(ref, sends, recvs)
         for copy in copies:
             copy.start()
         grid_copies.extend(copies)
 
-    for s in range(pieces + groups - 1):
-        for d in range(groups):
+    guest_copies = [
+        pltpu.make_async_remote_copy(
+            src_ref=orbital_values.at[place, pl.ds(k * cut, cut)],
+            dst_ref=guest_orbitals.at[place, pl.ds(k * cut, cut)],
+            send_sem=guest_send.at[k], recv_sem=guest_recv.at[k], device_id=at(g, host), device_id_type=MESH)
+        for k in range(pieces)
+    ]
+    guest_copies.append(pltpu.make_async_remote_copy(
+        src_ref=target_values.at[place, :], dst_ref=guest_targets.at[place, :],
+        send_sem=guest_send.at[pieces], recv_sem=guest_recv.at[pieces],
+        device_id=at(g, host), device_id_type=MESH))
+    pass_copies = [
+        spread_copies(guest_orbitals.at[place, pl.ds(k * cut, cut)], pass_send.at[k], pass_recv.at[k])
+        for k in range(pieces)
+    ]
+    pass_copies.append(spread_copies(guest_targets.at[place, :], pass_send.at[pieces], pass_recv.at[pieces]))
+
+    def pass_on(k):
+        @pl.when(hosting)
+        def _():
+            guest_copies[k].wait_recv()
+            for copy in pass_copies[k]:
+                copy.start()
+
+    for s in range(pieces + groups - 2):
+        for d in range(groups - 1):
             k = s - d
             if not 0 <= k < pieces:
                 continue
             if d > 0:
                 await_line(k, d)
-            elif k > 0:
-                own[k].wait()
-            if d < groups - 1 and s > 0:
+            if d == 0 and k > 0:
+                pl.when(jnp.logical_not(edge))(functools.partial(send_line, k, 0))
+            elif 0 < d < groups - 2:
                 send_line(k, d)
-        k = s - (groups - 1)
+        k = s - (groups - 2)
         if k < 0:
             continue
         columns = pl.ds(k * cut, cut)
-        values = jnp.zeros((count, cut), jnp.float32)
-        for chunk in range(groups):
-            values += pick(every_group[0], slab_start + chunk * rows, slab[chunk, :, columns])
-        orbital_values[place, columns] = values.astype(jnp.bfloat16)
+        def pick_chunk(chunk):
+            return pick(every_group[0], slab_start + chunk * rows, slab[chunk, :, columns])
+
+        piece_sum[...] = sum(pick_chunk(chunk) for chunk in range(1, last))
+
+        @pl.when(z != last)
+        def _():
+            piece_sum[...] += pick_chunk(0)
+
+        @pl.when(z != 0)
+        def _():
+            piece_sum[...] += pick_chunk(last)
+
+        @pl.when(edge)
+        def _():
+            far_copies[k].wait_recv()
+            piece_sum[...] += far_values[:, columns].astype(jnp.float32)
+
+        orbital_values[place, columns] = piece_sum[...].astype(jnp.bfloat16)
+        pl.when(edge)(guest_copies[k].start)
         spread(orbital_values.at[place, columns], grid_send.at[k], grid_recv.at[k])
         if k == 0:
             values = own_pick
@@ -151,47 +232,86 @@
                 pick_copies[step - 1].wait()
                 values += landed[step - 1].astype(jnp.float32)
             target_values[place, :] = values.astype(jnp.bfloat16)
+            pl.when(edge)(guest_copies[pieces].start)
             spread(target_values.at[place, :], value_send, value_recv)
+            pass_on(pieces)
+        else:
+            pass_on(k - 1)
+    pass_on(pieces - 1)
 
     own_weights.wait()
     for copy in grid_copies:
         copy.wait_recv()
 
-    def add_up(chunk):
-        total[...] = jnp.zeros_like(total)
-
+    def add(chunk, values, target_piece, kernel_ref, first_row):
         @pl.loop(0, slabs * count // WIDTH)
         def _(b):
             block = pl.ds(pl.multiple_of(b * WIDTH, WIDTH), WIDTH)
             products = lax.dot_general(
-                slab[chunk], orbital_values[block, :], (((1,), (1,)), ((), ())),
-                preferred_element_type=jnp.float32)
-            kernel_rows = weights[pl.ds(pl.multiple_of(chunk * rows, rows), rows), block]
+                slab[chunk], values[block, :], (((1,), (1,)), ((), ())), preferred_element_type=jnp.float32)
+            kernel_rows = kernel_ref[pl.ds(pl.multiple_of(first_row, rows), rows), block]
             weighted = (kernel_rows.astype(jnp.float32) * products).astype(jnp.bfloat16)
-            total[...] += jnp.dot(weighted, target_values[block, :], preferred_element_type=jnp.float32)
-
-    sum_copies = []
-    for n, step in enumerate(range(1, groups)):
-        chunk = other(z, step, groups)
-        add_up(chunk)
-        leaving[n] = total[...].astype(jnp.bfloat16)
-        copy = pltpu.make_async_remote_copy(
+            total[...] += jnp.dot(weighted, target_piece[block, :], preferred_element_type=jnp.float32)
+
+    def add_own(chunk):
+        total[...] = jnp.zeros_like(total)
+        add(chunk, orbital_values, target_values, weights, chunk * rows)
+
+    def sum_copy(n, chunk):
+        return pltpu.make_async_remote_copy(
             src_ref=leaving.at[n], dst_ref=arriving.at[n], send_sem=sum_send.at[n], recv_sem=sum_recv.at[n],
             device_id=at(g, chunk), device_id_type=MESH)
-        copy.start()
-        sum_copies.append(copy)
-    add_up(z)
-    summed = total[...]
-    for n, copy in enumerate(sum_copies):
-        copy.wait_recv()
-        summed += arriving[n].astype(jnp.float32)
-    out[...] = (-summed).astype(out.dtype)
+
+    def left_out(one, two):
+        return ((one == 0) & (two == last)) | ((one == last) & (two == 0))
+
+    middle = groups // 2
+    for step in [n for n in range(1, groups) if n != middle] + [middle]:
+        chunk = other(z, step, groups)
+
+        @pl.when(jnp.logical_not(left_out(z, chunk)))
+        def _():
+            add_own(chunk)
+
+            @pl.when(hosting & (chunk == guest_chunk))
+            def _():
+                for copies in pass_copies:
+                    for copy in copies:
+                        copy.wait_recv()
+                weight_copy.wait_recv()
+                add(guest_chunk, guest_orbitals, guest_targets, guest_weights, 0)
+
+            leaving[step - 1] = total[...].astype(jnp.bfloat16)
+            sum_copy(step - 1, chunk).start()
+
+    add_own(z)
+    for step in range(1, groups):
+        @pl.when(jnp.logical_not(left_out(z, other(z, groups - step, groups))))
+        def _():
+            sum_copy(step - 1, z).wait_recv()
+            total[...] += arriving[step - 1].astype(jnp.float32)
+    out[...] = (-total[...]).astype(out.dtype)
+
+    for step in range(1, groups):
+        chunk = other(z, step, groups)
+        pl.when(jnp.logical_not(left_out(z, chunk)))(sum_copy(step - 1, chunk).wait_send)
+
+    @pl.when(edge)
+    def _():
+        for copy in far_copies + guest_copies + [weight_copy]:
+            copy.wait_send()
+
+    @pl.when(hosting)
+    def _():
+        for copies in pass_copies:
+            for copy in copies:
+                copy.wait_send()
 
     for k in range(pieces):
-        for d in range(groups - 1):
+        for d in range(groups - 2):
             for valid, copy in (up(k, d), down(k, d)):
                 pl.when(valid)(copy.wait_send)
-    for copy in grid_copies + sum_copies:
+    for copy in grid_copies:
         copy.wait_send()
 
 
@@ -219,6 +339,12 @@
             pltpu.VMEM((rows, nj), jnp.float32),
             pltpu.VMEM((groups - 1, rows, nj), bf16),
             pltpu.VMEM((groups - 1, rows, nj), bf16),
+            pltpu.VMEM((count, norb // pieces), jnp.float32),
+            pltpu.VMEM((count, norb), bf16),
+            pltpu.VMEM((count, norb), bf16),
+            pltpu.VMEM((slabs * count, norb), bf16),
+            pltpu.VMEM((slabs * count, nj), bf16),
+            pltpu.VMEM((rows, potential.shape[1]), bf16),
             dma((pieces + 3,)),
             dma((pieces, groups - 1)),
             dma((pieces, groups - 1)),
@@ -233,6 +359,12 @@
             dma((slabs - 1,)),
             dma((groups - 1,)),
             dma((groups - 1,)),
+            dma((pieces,)),
+            dma((pieces,)),
+            dma((pieces + 2,)),
+            dma((pieces + 2,)),
+            dma((pieces + 1, slabs - 1)),
+            dma((pieces + 1, slabs - 1)),
         ],
         compiler_params=pltpu.CompilerParams(
             collective_id=0, has_side_effects=True, vmem_limit_bytes=60 * 1024 * 1024),

time: 114 us -> 127 us (1.11)
  the two profiles are of different devices: /device:TPU:31 before, /device:TPU:0 now
where the time goes in v2:
time: 127 us; the launch traced here: 126 us
  Pallas kernels  125 us (98%)
  local copies, waits for them, and re-layouts  1.67 us (1%)
    pallas_call x1, Pallas kernels, local(): pl.pallas_call(functools.partial(kernel, groups, slabs, pieces), out_shap...  125 us

profile of v2, /device:TPU:0, one launch (start us, length us, event | category | flops | bytes accessed | tf_op | source)
XLA Modules:
  0.0 126.4 jit_solution(2702827114385136714)
XLA Ops:
  0.0 124.7 %shard_map.46 = bf16[512,256]{1,0:T(8,128)(2,1)} custom-call(bf16[512,1024]{1,0:T(8,128)(2,1)} %orbitals.1, bf16[512,256]{1,0:T(8,128)(2,1)} %targets.1, s32[1,128]{1,0:T(1,128)} %points.1, bf16[2048,1024]{1,0:T(8,128)(2,1)} %potential.1), custom_call_target="tpu_custom_call" | custom-call | tf_op jit(solution)/shard_map/pallas_call | solution.py:325
  124.7 1.7 %copy.6 = bf16[512,256]{1,0:T(8,128)(2,1)} copy(bf16[512,256]{1,0:T(8,128)(2,1)} %shard_map.46) | data formatting | bytes 524288

commit v3 on v2

--- a/solution.py
+++ b/solution.py
@@ -133,10 +133,15 @@
             send_sem=far_send.at[k], recv_sem=far_recv.at[k], device_id=at(g, far), device_id_type=MESH)
         for k in range(pieces)
     ]
-    weight_copy = pltpu.make_async_remote_copy(
-        src_ref=potential.at[pl.ds(pl.multiple_of(far * rows, rows), rows), :], dst_ref=guest_weights,
-        send_sem=guest_send.at[pieces + 1], recv_sem=guest_recv.at[pieces + 1],
-        device_id=at(g, host), device_id_type=MESH)
+    share = rows // pieces
+    weight_copies = [
+        pltpu.make_async_remote_copy(
+            src_ref=potential.at[pl.ds(pl.multiple_of(far * rows + k * share, share), share), :],
+            dst_ref=guest_weights.at[pl.ds(k * share, share), :],
+            send_sem=guest_send.at[pieces + 1 + k], recv_sem=guest_recv.at[pieces + 1 + k],
+            device_id=at(g, host), device_id_type=MESH)
+        for k in range(pieces)
+    ]
 
     @pl.when(edge)
     def _():
@@ -147,7 +152,6 @@
             far_copies[k].start()
         for k in range(early, pieces):
             send_line(k, 0)
-        weight_copy.start()
 
     place = pl.ds(pl.multiple_of(g * count, count), count)
     grid_copies = []
@@ -224,7 +228,14 @@
             piece_sum[...] += far_values[:, columns].astype(jnp.float32)
 
         orbital_values[place, columns] = piece_sum[...].astype(jnp.bfloat16)
-        pl.when(edge)(guest_copies[k].start)
+
+        @pl.when(edge)
+        def _():
+            guest_copies[k].start()
+            for part in range(pieces):
+                if k == min(part, max(pieces - 2, 0)):
+                    weight_copies[part].start()
+
         spread(orbital_values.at[place, columns], grid_send.at[k], grid_recv.at[k])
         if k == 0:
             values = own_pick
@@ -278,7 +289,8 @@
                 for copies in pass_copies:
                     for copy in copies:
                         copy.wait_recv()
-                weight_copy.wait_recv()
+                for copy in weight_copies:
+                    copy.wait_recv()
                 add(guest_chunk, guest_orbitals, guest_targets, guest_weights, 0)
 
             leaving[step - 1] = total[...].astype(jnp.bfloat16)
@@ -298,7 +310,7 @@
 
     @pl.when(edge)
     def _():
-        for copy in far_copies + guest_copies + [weight_copy]:
+        for copy in far_copies + guest_copies + weight_copies:
             copy.wait_send()
 
     @pl.when(hosting)
@@ -361,8 +373,8 @@
             dma((groups - 1,)),
             dma((pieces,)),
             dma((pieces,)),
-            dma((pieces + 2,)),
-            dma((pieces + 2,)),
+            dma((2 * pieces + 1,)),
+            dma((2 * pieces + 1,)),
             dma((pieces + 1, slabs - 1)),
             dma((pieces + 1, slabs - 1)),
         ],

time: 127 us -> 116 us (0.913)
  Pallas kernels: 125 us -> 115 us
    pallas_call x1, Pallas kernels: 125 us -> 115 us  [local(): pl.pallas_call(functools.partial(kernel, groups, slabs, pieces), out_shap...]
where the time goes in v3:
time: 116 us
  Pallas kernels  115 us (99%)
  local copies, waits for them, and re-layouts  1.67 us (1%)
    pallas_call x1, Pallas kernels, local(): pl.pallas_call(functools.partial(kernel, groups, slabs, pieces), out_shap...  115 us

profile of v3, /device:TPU:0, one launch (start us, length us, event | category | flops | bytes accessed | tf_op | source)
XLA Modules:
  0.0 116.3 jit_solution(11628046996971593285)
XLA Ops:
  0.0 114.7 %shard_map.46 = bf16[512,256]{1,0:T(8,128)(2,1)} custom-call(bf16[512,1024]{1,0:T(8,128)(2,1)} %orbitals.1, bf16[512,256]{1,0:T(8,128)(2,1)} %targets.1, s32[1,128]{1,0:T(1,128)} %points.1, bf16[2048,1024]{1,0:T(8,128)(2,1)} %potential.1), custom_call_target="tpu_custom_call" | custom-call | tf_op jit(solution)/shard_map/pallas_call | solution.py:337
  114.7 1.7 %copy.6 = bf16[512,256]{1,0:T(8,128)(2,1)} copy(bf16[512,256]{1,0:T(8,128)(2,1)} %shard_map.46) | data formatting | bytes 524288
